TPU v7x, 32 devices: a whole 2x2x4 slice. The times are simulated.
32 devices in a mesh: snap: 16 (over z, y, core), zone: 2 (over x).
Axes of the slice: x: 2, y: 2, z: 4, core: 2. Of those that a mesh axis runs over, the one named last changes fastest.
Arguments:
- forward: bfloat16 [2048, 2048], P('zone', 'snap'), may hold values from -40 to 40, as said below
- adjoint: bfloat16 [2048, 2048], P('zone', 'snap'), may hold values from -0.125 to 0.125
Outputs:
- rotated: float32 [2048, 2048], P('snap', 'zone')
Inputs may be any that keep to these rules, and one draw needn't show every extreme that they name: `forward`: independent entries, each snapshot column with its own scale.
All inputs are finite; a program needn't handle non-finite values.
Results may differ from a plain program's by a relative error of at most 0.0003.
Values may be sent and summed in bfloat16 or wider, within the bound.
A program may use at most 64 MiB of HBM per device.

v0:
```python
import jax
import jax.numpy as jnp
from jax import lax
from jax.sharding import PartitionSpec as P

ROUNDS = 8


def shifted(value, axis, steps):
    count = lax.axis_size(axis)
    initial, last = (max(0, -steps), min(count, count - steps))
    return lax.ppermute(value, axis, [(source, source + steps) for source in range(initial, last)])


def highdot(a, b):
    return jnp.dot(a, b, precision=lax.Precision.HIGHEST, preferred_element_type=jnp.float32)


def pair_gram(pair):
    local = lax.dot_general(
        pair,
        pair,
        (((1,), (1,)), ((), ())),
        precision=lax.Precision.HIGHEST,
        preferred_element_type=jnp.float32,
    )
    return local


def orthogonalize(pair):
    gram = pair_gram(pair)
    scales = jnp.sqrt(jnp.diagonal(gram) + 1e-06)
    corr = gram / (scales[:, None] * scales[None, :])
    half_rows = corr.shape[0] // 2
    block = corr[:half_rows, half_rows:]
    spread = jnp.sqrt(jnp.sum(block * block))
    coupling = 0.5 * block / jnp.maximum(spread, 1.0)
    zeros = jnp.zeros((half_rows, half_rows), jnp.float32)
    skew = jnp.concatenate(
        [jnp.concatenate([zeros, coupling], axis=1), jnp.concatenate([-coupling.T, zeros], axis=1)],
        axis=0,
    )
    ident = jnp.eye(corr.shape[0], dtype=jnp.float32)
    minus = ident - skew
    square = highdot(minus, minus)
    normal = ident + highdot(skew.T, skew)
    factor = jnp.linalg.cholesky(normal)
    middle = lax.linalg.triangular_solve(factor, square, left_side=True, lower=True)
    rotation = lax.linalg.triangular_solve(
        factor, middle, left_side=True, lower=True, transpose_a=True
    )
    return highdot(rotation, pair)


def shards(forward, adjoint):
    partial_rows = lax.dot_general(
        forward,
        lax.all_gather(adjoint, "snap", axis=1, tiled=True),
        (((0,), (0,)), ((), ())),
        preferred_element_type=jnp.float32,
    )
    rows = lax.psum(partial_rows, "zone")
    half_rows = rows.shape[0] // 2
    top = rows[:half_rows]
    bottom = rows[half_rows:]
    place = lax.axis_index("snap")
    final_place = lax.axis_size("snap") - 1
    for rnd in range(ROUNDS):
        done = orthogonalize(jnp.concatenate([top, bottom], axis=0))
        top = done[:half_rows]
        bottom = done[half_rows:]
        if rnd + 1 < ROUNDS:
            outgoing = jnp.where(place == 0, bottom, top)
            came_right = shifted(outgoing, "snap", 1)
            came_left = shifted(bottom, "snap", -1)
            new_top = jnp.where(place == 0, top, came_right)
            new_bottom = jnp.where(place == final_place, top, came_left)
            top = new_top
            bottom = new_bottom
    result = jnp.concatenate([top, bottom], axis=0)
    width = result.shape[1] // lax.axis_size("zone")
    result = lax.dynamic_slice_in_dim(result, lax.axis_index("zone") * width, width, 1)
    return result


def solution(mesh):
    return jax.shard_map(
        shards,
        mesh=mesh,
        in_specs=(P("zone", "snap"), P("zone", "snap")),
        out_specs=P("snap", "zone"),
        check_vma=False,
    )
```

profile of v0, /device:TPU:1, one launch (start us, length us, event | category | flops | bytes accessed | tf_op | source)
XLA Modules:
  0.0 463.1 jit_solution(3175419123350176471)
XLA Ops:
  7.3 58.0 %all-gather.2.cloned.1.call-done = bf16[1024,2048]{1,0:T(8,128)(2,1)} async-done(((bf16[1024,128]{1,0:T(8,128)(2,1)}), bf16[1024,2048]{1,0:T(8,128)(2,1)}) %all-gather.2.cloned.1.call-update) | async-done | bytes 4194320 | tf_op jit(solution)/shard_map/all_gather | solution.py:58
  69.2 37.9 %all-reduce.18.cloned.1.call-done = f32[128,2048]{1,0:T(8,128)} async-done(((f32[128,2048]{1,0:T(8,128)}), f32[128,2048]{1,0:T(8,128)}) %all-reduce.18.cloned.1.call-update) | async-done | bytes 1048592 | tf_op jit(solution)/shard_map/psum | solution.py:62
  113.5 11.7 %cholesky.134 = f32[128,128]{1,0:T(8,128)S(1)} custom-call(f32[128,128]{1,0:T(8,128)S(1)} %fusion.69), custom_call_target="Cholesky" | custom-call | tf_op jit(solution)/shard_map/jit(cholesky)/cholesky | solution.py:47
  126.6 9.8 %custom-call.39 = f32[1,128,128]{1,2,0:T(8,128)S(1)} custom-call(f32[1,128,128]{2,1,0:T(8,128)S(1)} %fusion.14), custom_call_target="InvertDiagBlocksLowerTriangular" | custom-call | tf_op jit(solution)/shard_map/triangular_solve/custom-call.2 | solution.py:49
  144.1 9.3 %collective-permute-done = f32[64,2048]{1,0:T(8,128)S(1)} collective-permute-done((f32[64,2048]{1,0:T(8,128)S(1)}, f32[64,2048]{1,0:T(8,128)S(1)}, u32[]{:S(2)}, u32[]{:S(2)}) %collective-permute-start) | collective-permute-done | bytes 524320 | tf_op jit(solution)/shard_map/ppermute | solution.py:12
  158.3 11.7 %cholesky.145 = f32[128,128]{1,0:T(8,128)S(1)} custom-call(f32[128,128]{1,0:T(8,128)S(1)} %fusion.64), custom_call_target="Cholesky" | custom-call | tf_op jit(solution)/shard_map/jit(cholesky)/cholesky | solution.py:47
  171.3 9.8 %custom-call.41 = f32[1,128,128]{1,2,0:T(8,128)S(1)} custom-call(f32[1,128,128]{2,1,0:T(8,128)S(1)} %fusion.15), custom_call_target="InvertDiagBlocksLowerTriangular" | custom-call | tf_op jit(solution)/shard_map/triangular_solve/custom-call.2 | solution.py:49
  189.2 9.6 %collective-permute-done.2 = f32[64,2048]{1,0:T(8,128)S(1)} collective-permute-done((f32[64,2048]{1,0:T(8,128)S(1)}, f32[64,2048]{1,0:T(8,128)S(1)}, u32[]{:S(2)}, u32[]{:S(2)}) %collective-permute-start.2) | collective-permute-done | bytes 524320 | tf_op jit(solution)/shard_map/ppermute | solution.py:12
  203.7 11.7 %cholesky.156 = f32[128,128]{1,0:T(8,128)S(1)} custom-call(f32[128,128]{1,0:T(8,128)S(1)} %fusion.59), custom_call_target="Cholesky" | custom-call | tf_op jit(solution)/shard_map/jit(cholesky)/cholesky | solution.py:47
  216.8 9.8 %custom-call.43 = f32[1,128,128]{1,2,0:T(8,128)S(1)} custom-call(f32[1,128,128]{2,1,0:T(8,128)S(1)} %fusion.16), custom_call_target="InvertDiagBlocksLowerTriangular" | custom-call | tf_op jit(solution)/shard_map/triangular_solve/custom-call.2 | solution.py:49
  234.7 9.6 %collective-permute-done.4 = f32[64,2048]{1,0:T(8,128)S(1)} collective-permute-done((f32[64,2048]{1,0:T(8,128)S(1)}, f32[64,2048]{1,0:T(8,128)S(1)}, u32[]{:S(2)}, u32[]{:S(2)}) %collective-permute-start.4) | collective-permute-done | bytes 524320 | tf_op jit(solution)/shard_map/ppermute | solution.py:12
  249.1 11.7 %cholesky.167 = f32[128,128]{1,0:T(8,128)S(1)} custom-call(f32[128,128]{1,0:T(8,128)S(1)} %fusion.54), custom_call_target="Cholesky" | custom-call | tf_op jit(solution)/shard_map/jit(cholesky)/cholesky | solution.py:47
  262.2 9.8 %custom-call.45 = f32[1,128,128]{1,2,0:T(8,128)S(1)} custom-call(f32[1,128,128]{2,1,0:T(8,128)S(1)} %fusion.17), custom_call_target="InvertDiagBlocksLowerTriangular" | custom-call | tf_op jit(solution)/shard_map/triangular_solve/custom-call.2 | solution.py:49
  280.4 9.4 %collective-permute-done.6 = f32[64,2048]{1,0:T(8,128)S(1)} collective-permute-done((f32[64,2048]{1,0:T(8,128)S(1)}, f32[64,2048]{1,0:T(8,128)S(1)}, u32[]{:S(2)}, u32[]{:S(2)}) %collective-permute-start.6) | collective-permute-done | bytes 524320 | tf_op jit(solution)/shard_map/ppermute | solution.py:12
  294.6 11.7 %cholesky.178 = f32[128,128]{1,0:T(8,128)S(1)} custom-call(f32[128,128]{1,0:T(8,128)S(1)} %fusion.49), custom_call_target="Cholesky" | custom-call | tf_op jit(solution)/shard_map/jit(cholesky)/cholesky | solution.py:47
  307.6 9.8 %custom-call.47 = f32[1,128,128]{1,2,0:T(8,128)S(1)} custom-call(f32[1,128,128]{2,1,0:T(8,128)S(1)} %fusion.18), custom_call_target="InvertDiagBlocksLowerTriangular" | custom-call | tf_op jit(solution)/shard_map/triangular_solve/custom-call.2 | solution.py:49
  325.6 9.6 %collective-permute-done.8 = f32[64,2048]{1,0:T(8,128)S(1)} collective-permute-done((f32[64,2048]{1,0:T(8,128)S(1)}, f32[64,2048]{1,0:T(8,128)S(1)}, u32[]{:S(2)}, u32[]{:S(2)}) %collective-permute-start.8) | collective-permute-done | bytes 524320 | tf_op jit(solution)/shard_map/ppermute | solution.py:12
  340.0 11.7 %cholesky.189 = f32[128,128]{1,0:T(8,128)S(1)} custom-call(f32[128,128]{1,0:T(8,128)S(1)} %fusion.44), custom_call_target="Cholesky" | custom-call | tf_op jit(solution)/shard_map/jit(cholesky)/cholesky | solution.py:47
  353.1 9.8 %custom-call.49 = f32[1,128,128]{1,2,0:T(8,128)S(1)} custom-call(f32[1,128,128]{2,1,0:T(8,128)S(1)} %fusion.19), custom_call_target="InvertDiagBlocksLowerTriangular" | custom-call | tf_op jit(solution)/shard_map/triangular_solve/custom-call.2 | solution.py:49
  371.1 9.6 %collective-permute-done.10 = f32[64,2048]{1,0:T(8,128)S(1)} collective-permute-done((f32[64,2048]{1,0:T(8,128)S(1)}, f32[64,2048]{1,0:T(8,128)S(1)}, u32[]{:S(2)}, u32[]{:S(2)}) %collective-permute-start.10) | collective-permute-done | bytes 524320 | tf_op jit(solution)/shard_map/ppermute | solution.py:12
  385.5 11.7 %cholesky.200 = f32[128,128]{1,0:T(8,128)S(1)} custom-call(f32[128,128]{1,0:T(8,128)S(1)} %fusion.39), custom_call_target="Cholesky" | custom-call | tf_op jit(solution)/shard_map/jit(cholesky)/cholesky | solution.py:47
  398.5 9.8 %custom-call.51 = f32[1,128,128]{1,2,0:T(8,128)S(1)} custom-call(f32[1,128,128]{2,1,0:T(8,128)S(1)} %fusion.20), custom_call_target="InvertDiagBlocksLowerTriangular" | custom-call | tf_op jit(solution)/shard_map/triangular_solve/custom-call.2 | solution.py:49
  430.5 11.7 %cholesky.211 = f32[128,128]{1,0:T(8,128)S(1)} custom-call(f32[128,128]{1,0:T(8,128)S(1)} %fusion.34), custom_call_target="Cholesky" | custom-call | tf_op jit(solution)/shard_map/jit(cholesky)/cholesky | solution.py:47
  443.6 9.8 %custom-call.53 = f32[1,128,128]{1,2,0:T(8,128)S(1)} custom-call(f32[1,128,128]{2,1,0:T(8,128)S(1)} %fusion.21), custom_call_target="InvertDiagBlocksLowerTriangular" | custom-call | tf_op jit(solution)/shard_map/triangular_solve/custom-call.2 | solution.py:49
  (183 shorter events, 117.5 us)
Async XLA Ops:
  6.5 58.7 %copy-start = (bf16[1024,128]{1,0:T(8,128)(2,1)S(1)}, bf16[1024,128]{1,0:T(8,128)(2,1)}, u32[]{:S(2)}) copy-start(bf16[1024,128]{1,0:T(8,128)(2,1)} %param.7) | copy-start | bytes 786436
  6.5 58.7 %all-gather.2.cloned.1.call-start = ((), (), s32[]{:S(2)}) async-start(), calls=%async_computation | async-start | bytes 4456448 | tf_op jit(solution)/shard_map/all_gather | solution.py:58
  7.3 99.9 %all-reduce.18.cloned.1.call-start = ((), (), s32[]{:S(2)}) async-start(), calls=%async_computation.1 | async-start | bytes 2097152 | tf_op jit(solution)/shard_map/psum | solution.py:62
  107.2 29.7 %copy-start.1 = (f32[128,2048]{1,0:T(8,128)S(1)}, f32[128,2048]{1,0:T(8,128)}, u32[]{:S(2)}) copy-start(f32[128,2048]{1,0:T(8,128)} %all-reduce.18.cloned.1.call-done) | copy-start | bytes 3145732
  138.0 15.4 %collective-permute-start = (f32[64,2048]{1,0:T(8,128)S(1)}, f32[64,2048]{1,0:T(8,128)S(1)}, u32[]{:S(2)}, u32[]{:S(2)}) collective-permute-start(f32[64,2048]{1,0:T(8,128)S(1)} %get-tuple-element.50), channel_id=1, source_target_pairs={{0,2},{2,4},{4,6},{6,8},{8,10},{10,12},{12,14},{14,16},{16,18},{18... | collective-permute-start | bytes 1572872 | tf_op jit(solution)/shard_map/ppermute | solution.py:12
  141.7 11.7 %collective-permute-start.1 = (f32[64,2048]{1,0:T(8,128)S(1)}, f32[64,2048]{1,0:T(8,128)S(1)}, u32[]{:S(2)}, u32[]{:S(2)}) collective-permute-start(f32[64,2048]{1,0:T(8,128)S(1)} %get-tuple-element.51), channel_id=1, source_target_pairs={{2,0},{4,2},{6,4},{8,6},{10,8},{12,10},{14,12},{16,14},{18,16},{20... | collective-permute-start | bytes 1572872 | tf_op jit(solution)/shard_map/ppermute | solution.py:12
  182.7 16.1 %collective-permute-start.2 = (f32[64,2048]{1,0:T(8,128)S(1)}, f32[64,2048]{1,0:T(8,128)S(1)}, u32[]{:S(2)}, u32[]{:S(2)}) collective-permute-start(f32[64,2048]{1,0:T(8,128)S(1)} %get-tuple-element.46), channel_id=1, source_target_pairs={{0,2},{2,4},{4,6},{6,8},{8,10},{10,12},{12,14},{14,16},{16,18},{18... | collective-permute-start | bytes 1572872 | tf_op jit(solution)/shard_map/ppermute | solution.py:12
  187.1 11.7 %collective-permute-start.3 = (f32[64,2048]{1,0:T(8,128)S(1)}, f32[64,2048]{1,0:T(8,128)S(1)}, u32[]{:S(2)}, u32[]{:S(2)}) collective-permute-start(f32[64,2048]{1,0:T(8,128)S(1)} %get-tuple-element.47), channel_id=1, source_target_pairs={{2,0},{4,2},{6,4},{8,6},{10,8},{12,10},{14,12},{16,14},{18,16},{20... | collective-permute-start | bytes 1572872 | tf_op jit(solution)/shard_map/ppermute | solution.py:12
  228.2 16.1 %collective-permute-start.4 = (f32[64,2048]{1,0:T(8,128)S(1)}, f32[64,2048]{1,0:T(8,128)S(1)}, u32[]{:S(2)}, u32[]{:S(2)}) collective-permute-start(f32[64,2048]{1,0:T(8,128)S(1)} %get-tuple-element.42), channel_id=1, source_target_pairs={{0,2},{2,4},{4,6},{6,8},{8,10},{10,12},{12,14},{14,16},{16,18},{18... | collective-permute-start | bytes 1572872 | tf_op jit(solution)/shard_map/ppermute | solution.py:12
  232.6 11.7 %collective-permute-start.5 = (f32[64,2048]{1,0:T(8,128)S(1)}, f32[64,2048]{1,0:T(8,128)S(1)}, u32[]{:S(2)}, u32[]{:S(2)}) collective-permute-start(f32[64,2048]{1,0:T(8,128)S(1)} %get-tuple-element.43), channel_id=1, source_target_pairs={{2,0},{4,2},{6,4},{8,6},{10,8},{12,10},{14,12},{16,14},{18,16},{20... | collective-permute-start | bytes 1572872 | tf_op jit(solution)/shard_map/ppermute | solution.py:12
  273.6 16.1 %collective-permute-start.6 = (f32[64,2048]{1,0:T(8,128)S(1)}, f32[64,2048]{1,0:T(8,128)S(1)}, u32[]{:S(2)}, u32[]{:S(2)}) collective-permute-start(f32[64,2048]{1,0:T(8,128)S(1)} %get-tuple-element.38), channel_id=1, source_target_pairs={{0,2},{2,4},{4,6},{6,8},{8,10},{10,12},{12,14},{14,16},{16,18},{18... | collective-permute-start | bytes 1572872 | tf_op jit(solution)/shard_map/ppermute | solution.py:12
  278.0 11.7 %collective-permute-start.7 = (f32[64,2048]{1,0:T(8,128)S(1)}, f32[64,2048]{1,0:T(8,128)S(1)}, u32[]{:S(2)}, u32[]{:S(2)}) collective-permute-start(f32[64,2048]{1,0:T(8,128)S(1)} %get-tuple-element.39), channel_id=1, source_target_pairs={{2,0},{4,2},{6,4},{8,6},{10,8},{12,10},{14,12},{16,14},{18,16},{20... | collective-permute-start | bytes 1572872 | tf_op jit(solution)/shard_map/ppermute | solution.py:12
  319.1 16.1 %collective-permute-start.8 = (f32[64,2048]{1,0:T(8,128)S(1)}, f32[64,2048]{1,0:T(8,128)S(1)}, u32[]{:S(2)}, u32[]{:S(2)}) collective-permute-start(f32[64,2048]{1,0:T(8,128)S(1)} %get-tuple-element.34), channel_id=1, source_target_pairs={{0,2},{2,4},{4,6},{6,8},{8,10},{10,12},{12,14},{14,16},{16,18},{18... | collective-permute-start | bytes 1572872 | tf_op jit(solution)/shard_map/ppermute | solution.py:12
  323.5 11.7 %collective-permute-start.9 = (f32[64,2048]{1,0:T(8,128)S(1)}, f32[64,2048]{1,0:T(8,128)S(1)}, u32[]{:S(2)}, u32[]{:S(2)}) collective-permute-start(f32[64,2048]{1,0:T(8,128)S(1)} %get-tuple-element.35), channel_id=1, source_target_pairs={{2,0},{4,2},{6,4},{8,6},{10,8},{12,10},{14,12},{16,14},{18,16},{20... | collective-permute-start | bytes 1572872 | tf_op jit(solution)/shard_map/ppermute | solution.py:12
  364.5 16.1 %collective-permute-start.10 = (f32[64,2048]{1,0:T(8,128)S(1)}, f32[64,2048]{1,0:T(8,128)S(1)}, u32[]{:S(2)}, u32[]{:S(2)}) collective-permute-start(f32[64,2048]{1,0:T(8,128)S(1)} %get-tuple-element.30), channel_id=1, source_target_pairs={{0,2},{2,4},{4,6},{6,8},{8,10},{10,12},{12,14},{14,16},{16,18},{18... | collective-permute-start | bytes 1572872 | tf_op jit(solution)/shard_map/ppermute | solution.py:12
  368.9 11.7 %collective-permute-start.11 = (f32[64,2048]{1,0:T(8,128)S(1)}, f32[64,2048]{1,0:T(8,128)S(1)}, u32[]{:S(2)}, u32[]{:S(2)}) collective-permute-start(f32[64,2048]{1,0:T(8,128)S(1)} %get-tuple-element.31), channel_id=1, source_target_pairs={{2,0},{4,2},{6,4},{8,6},{10,8},{12,10},{14,12},{16,14},{18,16},{20... | collective-permute-start | bytes 1572872 | tf_op jit(solution)/shard_map/ppermute | solution.py:12
  410.0 15.7 %collective-permute-start.12 = (f32[64,2048]{1,0:T(8,128)S(1)}, f32[64,2048]{1,0:T(8,128)S(1)}, u32[]{:S(2)}, u32[]{:S(2)}) collective-permute-start(f32[64,2048]{1,0:T(8,128)S(1)} %get-tuple-element.26), channel_id=1, source_target_pairs={{0,2},{2,4},{4,6},{6,8},{8,10},{10,12},{12,14},{14,16},{16,18},{18... | collective-permute-start | bytes 1572872 | tf_op jit(solution)/shard_map/ppermute | solution.py:12
  414.4 11.4 %collective-permute-start.13 = (f32[64,2048]{1,0:T(8,128)S(1)}, f32[64,2048]{1,0:T(8,128)S(1)}, u32[]{:S(2)}, u32[]{:S(2)}) collective-permute-start(f32[64,2048]{1,0:T(8,128)S(1)} %get-tuple-element.27), channel_id=1, source_target_pairs={{2,0},{4,2},{6,4},{8,6},{10,8},{12,10},{14,12},{16,14},{18,16},{20... | collective-permute-start | bytes 1572872 | tf_op jit(solution)/shard_map/ppermute | solution.py:12
Sparse Core Ops, SparseCore 0:
  9.5 55.7 all-gather.1
  69.3 37.7 all-reduce.17
where the time goes:
time: 471 us; the launch traced here: 463 us
  other arithmetic  191 us (41%)
  waiting for transfers between devices  163 us (35%)
  starting transfers between devices  45.4 us (10%)
  matrix products  31.1 us (7%)
  between operations  20.4 us (4%)
  local copies, waits for them, and re-layouts  12.7 us (3%)
    another operation x24, other arithmetic, orthogonalize(): factor = jnp.linalg.cholesky(normal)  99.1 us
    another operation x16, other arithmetic, orthogonalize(): lax.linalg.triangular_solve(factor, middle, left_side=True, lower=True, t...  83.7 us
    ppermute x14, waiting for transfers between devices, shifted(): lax.ppermute(value, axis, [(source, source + steps) for source in range(i...  66.3 us
    all_gather x1, waiting for transfers between devices, shards(): lax.all_gather(adjoint, 'snap', axis=1, tiled=True)  58 us
    ppermute x14, starting transfers between devices, shifted(): lax.ppermute(value, axis, [(source, source + steps) for source in range(i...  45.4 us
    psum x1, waiting for transfers between devices, shards(): rows = lax.psum(partial_rows, 'zone')  37.9 us
    dot_general x24, matrix products, highdot(): jnp.dot(a, b, precision=lax.Precision.HIGHEST, preferred_element_type=jnp...  13.8 us
    gather x8, local copies, waits for them, and re-layouts, orthogonalize(): scales = jnp.sqrt(jnp.diagonal(gram) + 1e-06)  9.96 us
  transfers between devices with their start and end apart: 16, of which 9 were waited for; matrix products, arithmetic and copies ran while one was open for 0% of the time, Pallas kernels for 0%

commit v1 on v0

v1 whole, which is shorter than its diff:
```python
import functools

import numpy as np
import jax
import jax.numpy as jnp
from jax import lax
from jax.experimental import pallas as pl
from jax.experimental.pallas import tpu as pltpu
from jax.sharding import PartitionSpec as P

ROUNDS = 8
CHUNKS = 2
NN = (((1,), (0,)), ((), ()))
NT = (((1,), (1,)), ((), ()))


def inverse_coefficients(degree):
    cheb = np.polynomial.chebyshev.Chebyshev.basis(degree + 1).convert(kind=np.polynomial.Polynomial)
    shifted = cheb(np.polynomial.Polynomial([-1.0, 8.0]))
    residual = shifted / shifted(-1.0)
    quotient = (np.polynomial.Polynomial([1.0]) - residual) // np.polynomial.Polynomial([1.0, 1.0])
    return [float(c) for c in quotient.coef]


def split(a):
    high = a.astype(jnp.bfloat16)
    return high, (a - high.astype(jnp.float32)).astype(jnp.bfloat16)


def dot3(a, b, dims):
    (ah, al), (bh, bl) = a, b
    dot = functools.partial(lax.dot_general, dimension_numbers=dims, preferred_element_type=jnp.float32)
    return dot(ah, bh) + (dot(ah, bl) + dot(al, bh))


def rounds_kernel(n, nz, half, cw, rows_ref, out_ref, topbuf, botbuf, outtop, outbot, stats,
                  send_r, recv_t, send_l, recv_b, send_z, recv_z):
    s = lax.axis_index("snap")
    z = lax.axis_index("zone")
    coef = inverse_coefficients(6)

    barrier = pltpu.get_barrier_semaphore()

    @pl.when(s > 0)
    def _():
        pl.semaphore_signal(barrier, inc=1, device_id={"snap": s - 1}, device_id_type=pl.DeviceIdType.MESH)

    @pl.when(s < n - 1)
    def _():
        pl.semaphore_signal(barrier, inc=1, device_id={"snap": s + 1}, device_id_type=pl.DeviceIdType.MESH)

    for k in range(1, nz):
        pl.semaphore_signal(barrier, inc=1, device_id={"zone": lax.rem(z + k, nz)}, device_id_type=pl.DeviceIdType.MESH)

    for c in range(CHUNKS):
        topbuf[0, c] = rows_ref[0:half, c * cw:(c + 1) * cw]
        botbuf[0, c] = rows_ref[half:2 * half, c * cw:(c + 1) * cw]

    @pl.when((s > 0) & (s < n - 1))
    def _():
        pl.semaphore_wait(barrier, nz + 1)

    @pl.when((s == 0) | (s == n - 1))
    def _():
        pl.semaphore_wait(barrier, nz)

    def right_copy(r, c, src):
        return pltpu.make_async_remote_copy(
            src_ref=src.at[r, c], dst_ref=topbuf.at[r + 1, c], send_sem=send_r.at[r, c], recv_sem=recv_t.at[r + 1, c],
            device_id={"snap": jnp.minimum(s + 1, n - 1)}, device_id_type=pl.DeviceIdType.MESH)

    def left_copy(r, c):
        return pltpu.make_async_remote_copy(
            src_ref=outbot.at[r, c], dst_ref=botbuf.at[r + 1, c], send_sem=send_l.at[r, c], recv_sem=recv_b.at[r + 1, c],
            device_id={"snap": jnp.maximum(s - 1, 0)}, device_id_type=pl.DeviceIdType.MESH)

    def zone_copy(r, k):
        return pltpu.make_async_remote_copy(
            src_ref=stats.at[r, 0], dst_ref=stats.at[r, k], send_sem=send_z.at[r, k], recv_sem=recv_z.at[r, k],
            device_id={"zone": lax.rem(z + k, nz)}, device_id_type=pl.DeviceIdType.MESH)

    def rotate(r):
        block = None
        ones = jnp.ones((8, cw), jnp.bfloat16)
        for c in range(CHUNKS):
            top = topbuf[r, c]
            bottom = botbuf[r, c]
            part = dot3(split(top), split(bottom), NT)
            tops = jnp.sum(top * top, axis=1, keepdims=True)
            bh, bl = split(bottom * bottom)
            bots = (lax.dot_general(ones, bh, NT, preferred_element_type=jnp.float32)
                    + lax.dot_general(ones, bl, NT, preferred_element_type=jnp.float32))
            block, tsum, bsum = (part, tops, bots) if block is None else (block + part, tsum + tops, bsum + bots)
        stats[r, 0, 0:half, 0:half] = block
        stats[r, 0, 0:half, half:2 * half] = jnp.broadcast_to(tsum, (half, half))
        stats[r, 0, half:half + 8, 0:half] = bsum
        stats[r, 0, half:half + 8, half:2 * half] = bsum
        for k in range(1, nz):
            zone_copy(r, k).start()
        total = stats[r, 0]
        for k in range(1, nz):
            zone_copy(r, k).wait_recv()
            total = total + stats[r, k]
        tinv = 1.0 / jnp.sqrt(total[0:half, half:2 * half] + 1e-06)
        binv = 1.0 / jnp.sqrt(total[half:half + 1, 0:half] + 1e-06)
        corr = total[0:half, 0:half] * (tinv * binv)
        spread = jnp.sqrt(jnp.sum(corr * corr, keepdims=True))
        x = corr * (0.5 / jnp.maximum(spread, 1.0))
        xs = split(x)
        xts = split(x.T)
        ident = (lax.broadcasted_iota(jnp.int32, (half, half), 0)
                 == lax.broadcasted_iota(jnp.int32, (half, half), 1)).astype(jnp.float32)
        n1 = dot3(xs, xs, NT)
        n1s = split(n1)
        n2 = dot3(n1s, n1s, NN)
        n3 = dot3(split(n2), n1s, NN)
        upper = coef[3] * ident + coef[4] * n1 + coef[5] * n2 + coef[6] * n3
        inverse = coef[0] * ident + coef[1] * n1 + coef[2] * n2 + dot3(split(n3), split(upper), NN)
        invs = split(inverse)
        return xs, xts, invs

    def apply(r, c, parts):
        xs, xts, invs = parts
        top = topbuf[r, c]
        bottom = botbuf[r, c]
        v = top - dot3(xs, split(bottom), NN)
        w = dot3(invs, split(v), NN)
        return 2.0 * w - top, bottom + 2.0 * dot3(xts, split(w), NN)

    def step(r, carry):
        @pl.when((r > 0) & (s > 0))
        def _():
            for c in range(CHUNKS):
                right_copy(r - 1, c, outtop).wait_recv()

        @pl.when((r > 0) & (s < n - 1))
        def _():
            for c in range(CHUNKS):
                left_copy(r - 1, c).wait_recv()

        parts = rotate(r)
        for c in range(CHUNKS):
            top, bottom = apply(r, c, parts)
            outtop[r, c] = top
            outbot[r, c] = bottom

            @pl.when((s > 0) & (s < n - 1))
            def _():
                right_copy(r, c, outtop).start()

            @pl.when(s == 0)
            def _():
                right_copy(r, c, outbot).start()
                topbuf[r + 1, c] = outtop[r, c]

            @pl.when(s > 0)
            def _():
                left_copy(r, c).start()

            @pl.when(s == n - 1)
            def _():
                botbuf[r + 1, c] = outtop[r, c]
        return carry

    lax.fori_loop(0, ROUNDS - 1, step, 0)
    last = ROUNDS - 1

    @pl.when(s > 0)
    def _():
        for c in range(CHUNKS):
            right_copy(last - 1, c, outtop).wait_recv()

    @pl.when(s < n - 1)
    def _():
        for c in range(CHUNKS):
            left_copy(last - 1, c).wait_recv()

    parts = rotate(last)
    for c in range(CHUNKS):
        top, bottom = apply(last, c, parts)
        out_ref[0:half, c * cw:(c + 1) * cw] = top
        out_ref[half:2 * half, c * cw:(c + 1) * cw] = bottom

    def drain(r, carry):
        @pl.when(s < n - 1)
        def _():
            for c in range(CHUNKS):
                right_copy(r, c, outtop).wait_send()

        @pl.when(s > 0)
        def _():
            for c in range(CHUNKS):
                left_copy(r, c).wait_send()
        return carry

    lax.fori_loop(0, last, drain, 0)

    def drain_zone(r, carry):
        for k in range(1, nz):
            zone_copy(r, k).wait_send()
        return carry

    lax.fori_loop(0, ROUNDS, drain_zone, 0)


def run_rounds(rows, n, nz):
    height, width = rows.shape
    half = height // 2
    cw = width // CHUNKS
    return pl.pallas_call(
        functools.partial(rounds_kernel, n, nz, half, cw),
        out_shape=jax.ShapeDtypeStruct(rows.shape, jnp.float32),
        in_specs=[pl.BlockSpec(memory_space=pltpu.VMEM)],
        out_specs=pl.BlockSpec(memory_space=pltpu.VMEM),
        scratch_shapes=[
            pltpu.VMEM((ROUNDS, CHUNKS, half, cw), jnp.float32),
            pltpu.VMEM((ROUNDS, CHUNKS, half, cw), jnp.float32),
            pltpu.VMEM((ROUNDS - 1, CHUNKS, half, cw), jnp.float32),
            pltpu.VMEM((ROUNDS - 1, CHUNKS, half, cw), jnp.float32),
            pltpu.VMEM((ROUNDS, nz, half + 8, 2 * half), jnp.float32),
            pltpu.SemaphoreType.DMA((ROUNDS, CHUNKS)),
            pltpu.SemaphoreType.DMA((ROUNDS, CHUNKS)),
            pltpu.SemaphoreType.DMA((ROUNDS, CHUNKS)),
            pltpu.SemaphoreType.DMA((ROUNDS, CHUNKS)),
            pltpu.SemaphoreType.DMA((ROUNDS, nz)),
            pltpu.SemaphoreType.DMA((ROUNDS, nz)),
        ],
        compiler_params=pltpu.CompilerParams(
            collective_id=0, has_side_effects=True, vmem_limit_bytes=48 * 1024 * 1024),
    )(rows)


def solution(mesh):
    n, nz = mesh.shape["snap"], mesh.shape["zone"]

    def shards(forward, adjoint):
        partial_rows = lax.dot_general(
            forward,
            lax.all_gather(adjoint, "snap", axis=1, tiled=True),
            (((0,), (0,)), ((), ())),
            preferred_element_type=jnp.float32,
        )
        rows = lax.psum_scatter(partial_rows, "zone", scatter_dimension=1, tiled=True)
        return run_rounds(rows, n, nz)

    return jax.shard_map(
        shards,
        mesh=mesh,
        in_specs=(P("zone", "snap"), P("zone", "snap")),
        out_specs=P("snap", "zone"),
        check_vma=False,
    )
```

time: 471 us -> 174 us (0.37); the launches traced: 463 us -> 174 us
  other arithmetic: 191 us -> 0 us
  waiting for transfers between devices: 163 us -> 76.9 us
  Pallas kernels: 0 us -> 77.9 us
  starting transfers between devices: 45.4 us -> 0.04 us
  matrix products: 31.1 us -> 3.91 us
  local copies, waits for them, and re-layouts: 12.7 us -> 1.84 us
  between operations: 20.4 us -> 13.4 us
    another operation x40 -> x0, other arithmetic: 183 us -> none  [the longest x24 99.1 us: orthogonalize(): factor = jnp.linalg.cholesky(normal)]
    pallas_call x0 -> x1, Pallas kernels: none -> 77.9 us  [run_rounds(): pl.pallas_call(functools.partial(rounds_kernel, n, nz, half, cw), out_sha...]
    ppermute x14 -> x0, waiting for transfers between devices: 66.3 us -> none  [shifted(): lax.ppermute(value, axis, [(source, source + steps) for source in range(i...]
    ppermute x14 -> x0, starting transfers between devices: 45.4 us -> none  [shifted(): lax.ppermute(value, axis, [(source, source + steps) for source in range(i...]
    psum x1 -> x0, waiting for transfers between devices: 37.9 us -> none  [shards(): rows = lax.psum(partial_rows, 'zone')]
    dot_general x32 -> x0, matrix products: 23.3 us -> none  [the longest x24 13.8 us: highdot(): jnp.dot(a, b, precision=lax.Precision.HIGHEST, preferred_element_type=jnp...]
    reduce_scatter x0 -> x1, waiting for transfers between devices: none -> 18.2 us  [shards(): lax.psum_scatter(partial_rows, 'zone', scatter_dimension=1, tiled=True)]
    gather x8 -> x0, local copies, waits for them, and re-layouts: 9.96 us -> none  [orthogonalize(): scales = jnp.sqrt(jnp.diagonal(gram) + 1e-06)]
  transfers between devices with their start and end apart: 16 -> 2, of which waited for: 9 -> 2; matrix products, arithmetic and copies ran while one was open for 0% -> 0% of each run, Pallas kernels for 0% -> 0%
where the time goes in v1:
time: 174 us
  Pallas kernels  77.9 us (45%)
  waiting for transfers between devices  76.9 us (44%)
  between operations  13.4 us (8%)
  matrix products  3.91 us (2%)
  local copies, waits for them, and re-layouts  1.84 us (1%)
    pallas_call x1, Pallas kernels, run_rounds(): pl.pallas_call(functools.partial(rounds_kernel, n, nz, half, cw), out_sha...  77.9 us
    all_gather x1, waiting for transfers between devices, shards(): lax.all_gather(adjoint, 'snap', axis=1, tiled=True)  58 us
    reduce_scatter x1, waiting for transfers between devices, shards(): lax.psum_scatter(partial_rows, 'zone', scatter_dimension=1, tiled=True)  18.2 us
    dot_general x1, matrix products, shards(): lax.dot_general(forward, lax.all_gather(adjoint, 'snap', axis=1, tiled=Tr...  3.91 us
  transfers between devices with their start and end apart: 2, of which 2 were waited for; matrix products, arithmetic and copies ran while one was open for 0% of the time, Pallas kernels for 0%

profile of v1, /device:TPU:1, one launch (start us, length us, event | category | flops | bytes accessed | tf_op | source)
XLA Modules:
  0.0 174.0 jit_solution(16288785130882084429)
XLA Ops:
  6.5 0.0 copy-start
  6.5 0.0 all-gather.2.cloned.1.call-start
  6.5 0.7 all-gather.2.cloned.1.call-update
  7.3 0.0 reduce-scatter.2.cloned.1.call-start
  7.3 58.0 %all-gather.2.cloned.1.call-done = bf16[1024,2048]{1,0:T(8,128)(2,1)} async-done(((bf16[1024,128]{1,0:T(8,128)(2,1)}), bf16[1024,2048]{1,0:T(8,128)(2,1)}) %all-gather.2.cloned.1.call-update) | async-done | bytes 4194320 | tf_op jit(solution)/shard_map/all_gather | solution.py:239
  65.3 0.0 copy-done
  65.3 3.9 %fusion = f32[128,2048]{1,0:T(8,128)} fusion(bf16[1024,128]{1,0:T(8,128)(2,1)S(1)} %copy-done, bf16[1024,2048]{1,0:T(8,128)(2,1)} %all-gather.2.cloned.1.call-done), kind=kOutput, calls=%fused_computation | convolution fusion | flops 536870912 | bytes 5505024 | tf_op jit(solution)/shard_map/dot_general | solution.py:237
  69.2 0.0 reduce-scatter.2.cloned.1.call-update
  69.2 18.2 %reduce-scatter.2.cloned.1.call-done.rows_ref = f32[128,1024]{1,0:T(8,128)} async-done(((f32[128,2048]{1,0:T(8,128)}), f32[128,1024]{1,0:T(8,128)}) %reduce-scatter.2.cloned.1.call-update) | async-done | bytes 524304 | tf_op jit(solution)/shard_map/reduce_scatter | solution.py:243
  87.4 0.0 copy-start.1
  87.4 1.0 copy-done.1
  88.5 77.9 %shard_map.28 = f32[128,1024]{1,0:T(8,128)S(1)} custom-call(f32[128,1024]{1,0:T(8,128)S(1)} %copy-done.1), custom_call_target="tpu_custom_call" | custom-call | tf_op jit(solution)/shard_map/pallas_call | solution.py:210
  166.4 0.8 copy.4
Async XLA Ops:
  6.5 58.7 %copy-start = (bf16[1024,128]{1,0:T(8,128)(2,1)S(1)}, bf16[1024,128]{1,0:T(8,128)(2,1)}, u32[]{:S(2)}) copy-start(bf16[1024,128]{1,0:T(8,128)(2,1)} %param.2) | copy-start | bytes 786436
  6.5 58.7 %all-gather.2.cloned.1.call-start = ((), (), s32[]{:S(2)}) async-start(), calls=%async_computation.1 | async-start | bytes 4456448 | tf_op jit(solution)/shard_map/all_gather | solution.py:239
  7.3 80.2 %reduce-scatter.2.cloned.1.call-start = ((), (), s32[]{:S(2)}) async-start(), calls=%async_computation.2 | async-start | bytes 1572864 | tf_op jit(solution)/shard_map/reduce_scatter | solution.py:243
  87.4 1.0 copy-start.1
Sparse Core Ops, SparseCore 0:
  9.5 55.7 all-gather.1
  69.3 18.0 reduce-scatter.1

commit v2 on v1

--- a/solution.py
+++ b/solution.py
@@ -33,11 +33,21 @@
     return dot(ah, bh) + (dot(ah, bl) + dot(al, bh))
 
 
-def rounds_kernel(n, nz, half, cw, rows_ref, out_ref, topbuf, botbuf, outtop, outbot, stats,
-                  send_r, recv_t, send_l, recv_b, send_z, recv_z):
+def whole_kernel(n, nz, half, cw, fwd_ref, adj_ref, out_ref, topbuf, botbuf, outtop, outbot, stats,
+                 fwd_t, gathered, part, parts_in,
+                 send_r, recv_t, send_l, recv_b, send_z, recv_z, gsend, grecv, psend, precv):
     s = lax.axis_index("snap")
     z = lax.axis_index("zone")
     coef = inverse_coefficients(6)
+    length = n // 4
+    zc = s // 4
+    y = (s // 2) % 2
+    core = s % 2
+    across = s + 2 - 4 * y
+    sibling = s + 1 - 2 * core
+    across_sibling = across + 1 - 2 * core
+    per = n // nz
+    bw = 2 * half
 
     barrier = pltpu.get_barrier_semaphore()
 
@@ -49,20 +59,114 @@
     def _():
         pl.semaphore_signal(barrier, inc=1, device_id={"snap": s + 1}, device_id_type=pl.DeviceIdType.MESH)
 
+    @pl.when(zc > 0)
+    def _():
+        pl.semaphore_signal(barrier, inc=1, device_id={"snap": s - 4}, device_id_type=pl.DeviceIdType.MESH)
+
+    @pl.when(zc < length - 1)
+    def _():
+        pl.semaphore_signal(barrier, inc=1, device_id={"snap": s + 4}, device_id_type=pl.DeviceIdType.MESH)
+
+    pl.semaphore_signal(barrier, inc=1, device_id={"snap": across}, device_id_type=pl.DeviceIdType.MESH)
+    pl.semaphore_signal(barrier, inc=1, device_id={"snap": sibling}, device_id_type=pl.DeviceIdType.MESH)
     for k in range(1, nz):
         pl.semaphore_signal(barrier, inc=1, device_id={"zone": lax.rem(z + k, nz)}, device_id_type=pl.DeviceIdType.MESH)
-
-    for c in range(CHUNKS):
-        topbuf[0, c] = rows_ref[0:half, c * cw:(c + 1) * cw]
-        botbuf[0, c] = rows_ref[half:2 * half, c * cw:(c + 1) * cw]
-
-    @pl.when((s > 0) & (s < n - 1))
-    def _():
-        pl.semaphore_wait(barrier, nz + 1)
-
-    @pl.when((s == 0) | (s == n - 1))
-    def _():
-        pl.semaphore_wait(barrier, nz)
+    greeted = (nz + 1 + jnp.minimum(s, 1) + jnp.minimum(n - 1 - s, 1)
+               + jnp.minimum(zc, 1) + jnp.minimum(length - 1 - zc, 1))
+    pl.semaphore_wait(barrier, greeted)
+
+    pending = []
+
+    def guarded(guard, action):
+        if guard is None:
+            action()
+        else:
+            pl.when(guard)(action)
+
+    def both(a, b):
+        return b if a is None else a & b
+
+    def send_block(guard, src, kind, target):
+        def copy():
+            return pltpu.make_async_remote_copy(
+                src_ref=adj_ref if src is s else gathered.at[src], dst_ref=gathered.at[src],
+                send_sem=gsend.at[kind, src], recv_sem=grecv.at[src],
+                device_id={"snap": target}, device_id_type=pl.DeviceIdType.MESH)
+        guarded(guard, lambda: copy().start())
+        pending.append((guard, copy))
+
+    def await_block(guard, src):
+        guarded(guard, lambda: pltpu.make_async_remote_copy(
+            src_ref=gathered.at[src], dst_ref=gathered.at[src],
+            send_sem=gsend.at[0, src], recv_sem=grecv.at[src],
+            device_id={"snap": sibling}, device_id_type=pl.DeviceIdType.MESH).wait_recv())
+
+    def part_copy(src):
+        owner = src // per
+        slot = (owner - z + nz) % nz
+        return pltpu.make_async_remote_copy(
+            src_ref=part.at[src], dst_ref=parts_in.at[slot, src % per],
+            send_sem=psend.at[src], recv_sem=precv.at[slot, src % per],
+            device_id={"zone": owner}, device_id_type=pl.DeviceIdType.MESH)
+
+    def multiply(guard, src):
+        def action():
+            block = adj_ref[...] if src is s else gathered[src]
+            part[src] = lax.dot_general(fwd_t[...], block, NN, preferred_element_type=jnp.float32)
+
+            @pl.when(src // per != z)
+            def _():
+                part_copy(src).start()
+        guarded(guard, action)
+
+    def at_distance(base, t):
+        if t == 0:
+            return [(None, base, 0)]
+        return [(zc >= t, base - 4 * t, 1), (zc < length - t, base + 4 * t, -1)]
+
+    send_block(zc < length - 1, s, 0, jnp.minimum(s + 4, n - 1))
+    send_block(zc > 0, s, 1, jnp.maximum(s - 4, 0))
+    send_block(None, s, 2, across)
+    send_block(None, s, 3, sibling)
+    fwd_t[...] = fwd_ref[...].T
+    multiply(None, s)
+    for t in range(length + 1):
+        if 0 < t < length:
+            for guard, src, way in at_distance(s, t):
+                await_block(guard, src)
+                if way > 0:
+                    send_block(both(guard, zc < length - 1), src, 0, jnp.minimum(s + 4, n - 1))
+                else:
+                    send_block(both(guard, zc > 0), src, 1, jnp.maximum(s - 4, 0))
+                send_block(guard, src, 2, across)
+                send_block(guard, src, 3, sibling)
+            for guard, src, way in at_distance(s, t):
+                multiply(guard, src)
+        if t > 0:
+            for guard, src, way in at_distance(across, t - 1):
+                await_block(guard, src)
+                send_block(guard, src, 3, sibling)
+                multiply(guard, src)
+        if t < length:
+            for guard, src, way in at_distance(sibling, t):
+                await_block(guard, src)
+                multiply(guard, src)
+        if t > 0:
+            for guard, src, way in at_distance(across_sibling, t - 1):
+                await_block(guard, src)
+                multiply(guard, src)
+
+    for j in range(per):
+        rows = part[z * per + j]
+        for k in range(1, nz):
+            pltpu.make_async_remote_copy(
+                src_ref=parts_in.at[k, j], dst_ref=parts_in.at[k, j],
+                send_sem=psend.at[0], recv_sem=precv.at[k, j],
+                device_id={"zone": lax.rem(z + 1, nz)}, device_id_type=pl.DeviceIdType.MESH).wait_recv()
+            rows = rows + parts_in[k, j]
+        c, at = divmod(j * bw, cw)
+        topbuf[0, c, :, at:at + bw] = rows[0:half]
+        botbuf[0, c, :, at:at + bw] = rows[half:bw]
 
     def right_copy(r, c, src):
         return pltpu.make_async_remote_copy(
@@ -202,46 +306,55 @@
 
     lax.fori_loop(0, ROUNDS, drain_zone, 0)
 
-
-def run_rounds(rows, n, nz):
-    height, width = rows.shape
-    half = height // 2
-    cw = width // CHUNKS
-    return pl.pallas_call(
-        functools.partial(rounds_kernel, n, nz, half, cw),
-        out_shape=jax.ShapeDtypeStruct(rows.shape, jnp.float32),
-        in_specs=[pl.BlockSpec(memory_space=pltpu.VMEM)],
-        out_specs=pl.BlockSpec(memory_space=pltpu.VMEM),
-        scratch_shapes=[
-            pltpu.VMEM((ROUNDS, CHUNKS, half, cw), jnp.float32),
-            pltpu.VMEM((ROUNDS, CHUNKS, half, cw), jnp.float32),
-            pltpu.VMEM((ROUNDS - 1, CHUNKS, half, cw), jnp.float32),
-            pltpu.VMEM((ROUNDS - 1, CHUNKS, half, cw), jnp.float32),
-            pltpu.VMEM((ROUNDS, nz, half + 8, 2 * half), jnp.float32),
-            pltpu.SemaphoreType.DMA((ROUNDS, CHUNKS)),
-            pltpu.SemaphoreType.DMA((ROUNDS, CHUNKS)),
-            pltpu.SemaphoreType.DMA((ROUNDS, CHUNKS)),
-            pltpu.SemaphoreType.DMA((ROUNDS, CHUNKS)),
-            pltpu.SemaphoreType.DMA((ROUNDS, nz)),
-            pltpu.SemaphoreType.DMA((ROUNDS, nz)),
-        ],
-        compiler_params=pltpu.CompilerParams(
-            collective_id=0, has_side_effects=True, vmem_limit_bytes=48 * 1024 * 1024),
-    )(rows)
+    for guard, copy in pending:
+        guarded(guard, lambda: copy().wait_send())
+
+    def drain_parts(src, carry):
+        @pl.when(src // per != z)
+        def _():
+            part_copy(src).wait_send()
+        return carry
+
+    lax.fori_loop(0, n, drain_parts, 0)
 
 
 def solution(mesh):
     n, nz = mesh.shape["snap"], mesh.shape["zone"]
 
     def shards(forward, adjoint):
-        partial_rows = lax.dot_general(
-            forward,
-            lax.all_gather(adjoint, "snap", axis=1, tiled=True),
-            (((0,), (0,)), ((), ())),
-            preferred_element_type=jnp.float32,
-        )
-        rows = lax.psum_scatter(partial_rows, "zone", scatter_dimension=1, tiled=True)
-        return run_rounds(rows, n, nz)
+        zones, bw = forward.shape
+        half = bw // 2
+        width = bw * n // nz
+        cw = width // CHUNKS
+        return pl.pallas_call(
+            functools.partial(whole_kernel, n, nz, half, cw),
+            out_shape=jax.ShapeDtypeStruct((bw, width), jnp.float32),
+            in_specs=[pl.BlockSpec(memory_space=pltpu.VMEM)] * 2,
+            out_specs=pl.BlockSpec(memory_space=pltpu.VMEM),
+            scratch_shapes=[
+                pltpu.VMEM((ROUNDS, CHUNKS, half, cw), jnp.float32),
+                pltpu.VMEM((ROUNDS, CHUNKS, half, cw), jnp.float32),
+                pltpu.VMEM((ROUNDS - 1, CHUNKS, half, cw), jnp.float32),
+                pltpu.VMEM((ROUNDS - 1, CHUNKS, half, cw), jnp.float32),
+                pltpu.VMEM((ROUNDS, nz, half + 8, 2 * half), jnp.float32),
+                pltpu.VMEM((bw, zones), jnp.bfloat16),
+                pltpu.VMEM((n, zones, bw), jnp.bfloat16),
+                pltpu.VMEM((n, bw, bw), jnp.float32),
+                pltpu.VMEM((nz, n // nz, bw, bw), jnp.float32),
+                pltpu.SemaphoreType.DMA((ROUNDS, CHUNKS)),
+                pltpu.SemaphoreType.DMA((ROUNDS, CHUNKS)),
+                pltpu.SemaphoreType.DMA((ROUNDS, CHUNKS)),
+                pltpu.SemaphoreType.DMA((ROUNDS, CHUNKS)),
+                pltpu.SemaphoreType.DMA((ROUNDS, nz)),
+                pltpu.SemaphoreType.DMA((ROUNDS, nz)),
+                pltpu.SemaphoreType.DMA((4, n)),
+                pltpu.SemaphoreType.DMA((n,)),
+                pltpu.SemaphoreType.DMA((n,)),
+                pltpu.SemaphoreType.DMA((nz, n // nz)),
+            ],
+            compiler_params=pltpu.CompilerParams(
+                collective_id=0, has_side_effects=True, vmem_limit_bytes=48 * 1024 * 1024),
+        )(forward, adjoint)
 
     return jax.shard_map(
         shards,

time: 174 us -> 115 us (0.66)
  waiting for transfers between devices: 76.9 us -> 0 us
  Pallas kernels: 77.9 us -> 112 us
  between operations: 13.4 us -> 0.01 us
  matrix products: 3.91 us -> 0 us
    all_gather x1 -> x0, waiting for transfers between devices: 58 us -> none  [shards(): lax.all_gather(adjoint, 'snap', axis=1, tiled=True)]
    pallas_call x1, Pallas kernels: 77.9 us -> 112 us  [shards(): pl.pallas_call(functools.partial(whole_kernel, n, nz, half, cw), out_shap...]
    reduce_scatter x1 -> x0, waiting for transfers between devices: 18.2 us -> none  [shards(): lax.psum_scatter(partial_rows, 'zone', scatter_dimension=1, tiled=True)]
    dot_general x1 -> x0, matrix products: 3.91 us -> none  [shards(): lax.dot_general(forward, lax.all_gather(adjoint, 'snap', axis=1, tiled=Tr...]
  transfers between devices with their start and end apart: 2 -> 0, of which waited for: 2 -> 0; matrix products, arithmetic and copies ran while one was open for 0% -> 0% of each run, Pallas kernels for 0% -> 0%
where the time goes in v2:
time: 115 us; the launch traced here: 114 us
  Pallas kernels  112 us (97%)
  local copies, waits for them, and re-layouts  2.69 us (2%)
    pallas_call x1, Pallas kernels, shards(): pl.pallas_call(functools.partial(whole_kernel, n, nz, half, cw), out_shap...  112 us
    unnamed x5, local copies, waits for them, and re-layouts  2.69 us

profile of v2, /device:TPU:1, one launch (start us, length us, event | category | flops | bytes accessed | tf_op | source)
XLA Modules:
  0.0 114.2 jit_solution(16423702354192011965)
XLA Ops:
  0.0 0.0 copy-start
  0.0 0.9 copy-done
  1.0 0.0 copy-start.1
  1.0 0.9 copy-done.1
  1.9 111.5 %shard_map.28 = f32[128,1024]{1,0:T(8,128)S(1)} custom-call(bf16[1024,128]{1,0:T(8,128)(2,1)S(1)} %copy-done, bf16[1024,128]{1,0:T(8,128)(2,1)S(1)} %copy-done.1), custom_call_target="tpu_custom_call" | custom-call | tf_op jit(solution)/shard_map/pallas_call | solution.py:329
  113.4 0.8 copy.4
Async XLA Ops:
  0.0 0.9 copy-start
  1.0 0.9 copy-start.1

commit v3 on v2

--- a/solution.py
+++ b/solution.py
@@ -31,6 +31,10 @@
     (ah, al), (bh, bl) = a, b
     dot = functools.partial(lax.dot_general, dimension_numbers=dims, preferred_element_type=jnp.float32)
     return dot(ah, bh) + (dot(ah, bl) + dot(al, bh))
+
+
+def dot1(a, b):
+    return lax.dot_general(a, b, NT, preferred_element_type=jnp.float32)
 
 
 def whole_kernel(n, nz, half, cw, fwd_ref, adj_ref, out_ref, topbuf, botbuf, outtop, outbot, stats,
@@ -48,6 +52,7 @@
     across_sibling = across + 1 - 2 * core
     per = n // nz
     bw = 2 * half
+    short = half // 2
 
     barrier = pltpu.get_barrier_semaphore()
 
@@ -183,31 +188,72 @@
             src_ref=stats.at[r, 0], dst_ref=stats.at[r, k], send_sem=send_z.at[r, k], recv_sem=recv_z.at[r, k],
             device_id={"zone": lax.rem(z + k, nz)}, device_id_type=pl.DeviceIdType.MESH)
 
+    def settle(r):
+        @pl.when(r == 0)
+        def _():
+            for guard, copy in pending:
+                guarded(guard, lambda: copy().wait_send())
+
+            def parts_sent(src, carry):
+                @pl.when(src // per != z)
+                def _():
+                    part_copy(src).wait_send()
+                return carry
+
+            lax.fori_loop(0, n, parts_sent, 0)
+
+        @pl.when((r > 0) & (s < n - 1))
+        def _():
+            for c in range(CHUNKS):
+                right_copy(r - 1, c, outtop).wait_send()
+
+        @pl.when((r > 0) & (s > 0))
+        def _():
+            for c in range(CHUNKS):
+                left_copy(r - 1, c).wait_send()
+
+        @pl.when(r > 0)
+        def _():
+            for k in range(1, nz):
+                zone_copy(r - 1, k).wait_send()
+
+    def take(r, c):
+        @pl.when((r > 0) & (s > 0))
+        def _():
+            right_copy(r - 1, c, outtop).wait_recv()
+
+        @pl.when((r > 0) & (s < n - 1))
+        def _():
+            left_copy(r - 1, c).wait_recv()
+
     def rotate(r):
         block = None
         ones = jnp.ones((8, cw), jnp.bfloat16)
         for c in range(CHUNKS):
+            take(r, c)
             top = topbuf[r, c]
             bottom = botbuf[r, c]
             part = dot3(split(top), split(bottom), NT)
-            tops = jnp.sum(top * top, axis=1, keepdims=True)
+            th, tl = split(top * top)
+            tops = dot1(ones, th) + dot1(ones, tl)
             bh, bl = split(bottom * bottom)
-            bots = (lax.dot_general(ones, bh, NT, preferred_element_type=jnp.float32)
-                    + lax.dot_general(ones, bl, NT, preferred_element_type=jnp.float32))
+            bots = dot1(ones, bh) + dot1(ones, bl)
             block, tsum, bsum = (part, tops, bots) if block is None else (block + part, tsum + tops, bsum + bots)
-        stats[r, 0, 0:half, 0:half] = block
-        stats[r, 0, 0:half, half:2 * half] = jnp.broadcast_to(tsum, (half, half))
-        stats[r, 0, half:half + 8, 0:half] = bsum
-        stats[r, 0, half:half + 8, half:2 * half] = bsum
+        stats[r, 0, 0:short, 0:half] = block[0:short]
+        stats[r, 0, 0:short, half:2 * half] = block[short:half]
+        stats[r, 0, short:short + 8, 0:half] = tsum
+        stats[r, 0, short:short + 8, half:2 * half] = bsum
         for k in range(1, nz):
             zone_copy(r, k).start()
+        settle(r)
         total = stats[r, 0]
         for k in range(1, nz):
             zone_copy(r, k).wait_recv()
             total = total + stats[r, k]
-        tinv = 1.0 / jnp.sqrt(total[0:half, half:2 * half] + 1e-06)
-        binv = 1.0 / jnp.sqrt(total[half:half + 1, 0:half] + 1e-06)
-        corr = total[0:half, 0:half] * (tinv * binv)
+        inv = 1.0 / jnp.sqrt(total[short:short + 1] + 1e-06)
+        tinv = jnp.broadcast_to(inv[:, 0:half], (half, half)).T
+        gram = jnp.concatenate([total[0:short, 0:half], total[0:short, half:2 * half]], axis=0)
+        corr = gram * (tinv * inv[:, half:2 * half])
         spread = jnp.sqrt(jnp.sum(corr * corr, keepdims=True))
         x = corr * (0.5 / jnp.maximum(spread, 1.0))
         xs = split(x)
@@ -217,31 +263,21 @@
         n1 = dot3(xs, xs, NT)
         n1s = split(n1)
         n2 = dot3(n1s, n1s, NN)
+        mixed = [topbuf[r, c] - dot3(xs, split(botbuf[r, c]), NN) for c in range(CHUNKS)]
         n3 = dot3(split(n2), n1s, NN)
         upper = coef[3] * ident + coef[4] * n1 + coef[5] * n2 + coef[6] * n3
         inverse = coef[0] * ident + coef[1] * n1 + coef[2] * n2 + dot3(split(n3), split(upper), NN)
         invs = split(inverse)
-        return xs, xts, invs
+        return xts, invs, mixed
 
     def apply(r, c, parts):
-        xs, xts, invs = parts
+        xts, invs, mixed = parts
         top = topbuf[r, c]
         bottom = botbuf[r, c]
-        v = top - dot3(xs, split(bottom), NN)
-        w = dot3(invs, split(v), NN)
+        w = dot3(invs, split(mixed[c]), NN)
         return 2.0 * w - top, bottom + 2.0 * dot3(xts, split(w), NN)
 
     def step(r, carry):
-        @pl.when((r > 0) & (s > 0))
-        def _():
-            for c in range(CHUNKS):
-                right_copy(r - 1, c, outtop).wait_recv()
-
-        @pl.when((r > 0) & (s < n - 1))
-        def _():
-            for c in range(CHUNKS):
-                left_copy(r - 1, c).wait_recv()
-
         parts = rotate(r)
         for c in range(CHUNKS):
             top, bottom = apply(r, c, parts)
@@ -269,53 +305,14 @@
     lax.fori_loop(0, ROUNDS - 1, step, 0)
     last = ROUNDS - 1
 
-    @pl.when(s > 0)
-    def _():
-        for c in range(CHUNKS):
-            right_copy(last - 1, c, outtop).wait_recv()
-
-    @pl.when(s < n - 1)
-    def _():
-        for c in range(CHUNKS):
-            left_copy(last - 1, c).wait_recv()
-
     parts = rotate(last)
     for c in range(CHUNKS):
         top, bottom = apply(last, c, parts)
         out_ref[0:half, c * cw:(c + 1) * cw] = top
         out_ref[half:2 * half, c * cw:(c + 1) * cw] = bottom
 
-    def drain(r, carry):
-        @pl.when(s < n - 1)
-        def _():
-            for c in range(CHUNKS):
-                right_copy(r, c, outtop).wait_send()
-
-        @pl.when(s > 0)
-        def _():
-            for c in range(CHUNKS):
-                left_copy(r, c).wait_send()
-        return carry
-
-    lax.fori_loop(0, last, drain, 0)
-
-    def drain_zone(r, carry):
-        for k in range(1, nz):
-            zone_copy(r, k).wait_send()
-        return carry
-
-    lax.fori_loop(0, ROUNDS, drain_zone, 0)
-
-    for guard, copy in pending:
-        guarded(guard, lambda: copy().wait_send())
-
-    def drain_parts(src, carry):
-        @pl.when(src // per != z)
-        def _():
-            part_copy(src).wait_send()
-        return carry
-
-    lax.fori_loop(0, n, drain_parts, 0)
+    for k in range(1, nz):
+        zone_copy(last, k).wait_send()
 
 
 def solution(mesh):
@@ -336,7 +333,7 @@
                 pltpu.VMEM((ROUNDS, CHUNKS, half, cw), jnp.float32),
                 pltpu.VMEM((ROUNDS - 1, CHUNKS, half, cw), jnp.float32),
                 pltpu.VMEM((ROUNDS - 1, CHUNKS, half, cw), jnp.float32),
-                pltpu.VMEM((ROUNDS, nz, half + 8, 2 * half), jnp.float32),
+                pltpu.VMEM((ROUNDS, nz, half // 2 + 8, 2 * half), jnp.float32),
                 pltpu.VMEM((bw, zones), jnp.bfloat16),
                 pltpu.VMEM((n, zones, bw), jnp.bfloat16),
                 pltpu.VMEM((n, bw, bw), jnp.float32),

time: 115 us -> 112 us (0.974)
  Pallas kernels: 112 us -> 109 us
    pallas_call x1, Pallas kernels: 112 us -> 109 us  [shards(): pl.pallas_call(functools.partial(whole_kernel, n, nz, half, cw), out_shap...]
where the time goes in v3:
time: 112 us
  Pallas kernels  109 us (97%)
  local copies, waits for them, and re-layouts  2.69 us (2%)
    pallas_call x1, Pallas kernels, shards(): pl.pallas_call(functools.partial(whole_kernel, n, nz, half, cw), out_shap...  109 us
    unnamed x5, local copies, waits for them, and re-layouts  2.69 us

profile of v3, /device:TPU:1, one launch (start us, length us, event | category | flops | bytes accessed | tf_op | source)
XLA Modules:
  0.0 111.9 jit_solution(13310921685085358437)
XLA Ops:
  0.0 0.0 copy-start
  0.0 0.9 copy-done
  1.0 0.0 copy-start.1
  1.0 0.9 copy-done.1
  1.9 109.2 %shard_map.28 = f32[128,1024]{1,0:T(8,128)S(1)} custom-call(bf16[1024,128]{1,0:T(8,128)(2,1)S(1)} %copy-done, bf16[1024,128]{1,0:T(8,128)(2,1)S(1)} %copy-done.1), custom_call_target="tpu_custom_call" | custom-call | tf_op jit(solution)/shard_map/pallas_call | solution.py:326
  111.2 0.8 copy.4
Async XLA Ops:
  0.0 0.9 copy-start
  1.0 0.9 copy-start.1

commit v4 on v3

--- a/solution.py
+++ b/solution.py
@@ -9,7 +9,7 @@
 from jax.sharding import PartitionSpec as P
 
 ROUNDS = 8
-CHUNKS = 2
+CHUNKS = 4
 NN = (((1,), (0,)), ((), ()))
 NT = (((1,), (1,)), ((), ()))
 

time: 112 us -> 112 us (level)
  no operation moved by 1% of the time
where the time goes in v4:
time: 112 us
  Pallas kernels  109 us (97%)
  local copies, waits for them, and re-layouts  2.69 us (2%)
    pallas_call x1, Pallas kernels, shards(): pl.pallas_call(functools.partial(whole_kernel, n, nz, half, cw), out_shap...  109 us
    unnamed x5, local copies, waits for them, and re-layouts  2.69 us

profile of v4, /device:TPU:1, one launch (start us, length us, event | category | flops | bytes accessed | tf_op | source)
XLA Modules:
  0.0 111.7 jit_solution(8534328322016290165)
XLA Ops:
  0.0 0.0 copy-start
  0.0 0.9 copy-done
  1.0 0.0 copy-start.1
  1.0 0.9 copy-done.1
  1.9 109.0 %shard_map.28 = f32[128,1024]{1,0:T(8,128)S(1)} custom-call(bf16[1024,128]{1,0:T(8,128)(2,1)S(1)} %copy-done, bf16[1024,128]{1,0:T(8,128)(2,1)S(1)} %copy-done.1), custom_call_target="tpu_custom_call" | custom-call | tf_op jit(solution)/shard_map/pallas_call | solution.py:326
  110.9 0.8 copy.4
Async XLA Ops:
  0.0 0.9 copy-start
  1.0 0.9 copy-start.1
